TPU v7x, 32 devices: a whole 2x2x4 slice. The times are simulated.
32 devices in a mesh: depth: 4 (over z), tile: 8 (over y, x, core).
Axes of the slice: x: 2, y: 2, z: 4, core: 2. Of those that a mesh axis runs over, the one named last changes fastest.
Arguments:
- density: bfloat16 [32, 256, 1024], P('depth', None, 'tile'), may hold values from 0 to 1
- view_zoom: float32 [2], replicated, may hold values from 0.5 to 0.9
- view_shift: float32 [2], replicated, may hold values from 0 to 16
- tf_weights: float32 [2, 4, 8], replicated, may hold values from 0.25 to 2
- perm_order: int32 [2, 4], replicated, may hold values from 0 to 3, each once within a row
Outputs:
- image: float32 [2, 4, 256, 1024], P(None, None, 'depth', 'tile')
All inputs are finite; a program needn't handle non-finite values.
Results may differ from a plain program's by a relative error of at most 0.0028.
Values may be sent and summed in bfloat16 or wider, within the bound.
A program may use at most 64 MiB of HBM per device.

v0:
```python
import jax
import jax.numpy as jnp
from jax import lax
from jax.sharding import PartitionSpec as P

RADIUS = 8


OCCLUSION_GAIN = 1.5
EXTINCTION = 0.5


def with_halo(block, sides, width):
    for axis, dim in sides:
        count = lax.axis_size(axis)
        forward = [(i, i + 1) for i in range(count - 1)]
        backward = [(target, source) for source, target in forward]
        low = lax.ppermute(
            lax.slice_in_dim(block, block.shape[dim] - width, None, axis=dim), axis, forward
        )
        high = lax.ppermute(lax.slice_in_dim(block, 0, width, axis=dim), axis, backward)
        block = jnp.concatenate([low, block, high], axis=dim)
    return block


def blur_weights(radius):
    offsets = jnp.arange(-radius, radius + 1, dtype=jnp.float32)
    tap_weights = jnp.exp(-offsets * offsets / 72.0)
    return tap_weights / jnp.sum(tap_weights)


def occlusion_of(padded, radius, depth_cells, width_cells):
    tap_weights = blur_weights(radius)
    tap_count = 2 * radius + 1
    row_count = padded.shape[1]
    along_depth = tap_weights[0] * padded[0:depth_cells].astype(jnp.float32)
    for tap_index in range(1, tap_count):
        along_depth = along_depth + tap_weights[tap_index] * padded[
            tap_index : tap_index + depth_cells
        ].astype(jnp.float32)
    padded_rows = jnp.pad(along_depth, ((0, 0), (radius, radius), (0, 0)))
    along_rows = tap_weights[0] * padded_rows[:, 0:row_count]
    for tap_index in range(1, tap_count):
        along_rows = (
            along_rows + tap_weights[tap_index] * padded_rows[:, tap_index : tap_index + row_count]
        )
    along_width = tap_weights[0] * along_rows[:, :, 0:width_cells]
    for tap_index in range(1, tap_count):
        along_width = (
            along_width
            + tap_weights[tap_index] * along_rows[:, :, tap_index : tap_index + width_cells]
        )
    return jnp.exp(-OCCLUSION_GAIN * along_width).astype(jnp.bfloat16)


def resample_table(view_zoom, view_shift, row_count):
    pixel_pos = jnp.arange(row_count, dtype=jnp.float32)
    where_at = view_zoom[:, None] * pixel_pos[None, :] + view_shift[:, None]
    cell_pos = jnp.arange(row_count, dtype=jnp.float32)
    interp_table = jnp.maximum(0.0, 1.0 - jnp.abs(where_at[:, :, None] - cell_pos[None, None, :]))
    return interp_table.reshape(-1, row_count).astype(jnp.bfloat16)


def render_slab(slab_density, slab_shade, interp_table, tf_weights, depth_total):
    view_count = tf_weights.shape[0]
    basis_count = tf_weights.shape[2]
    row_count = slab_density.shape[1]
    width_cells = slab_density.shape[2]

    def one_slice(state_pair, cell_pair):
        colour, passing = state_pair
        density_rows, shade_rows = cell_pair
        stacked = jnp.concatenate([density_rows, shade_rows], axis=1)
        sampled = jnp.dot(interp_table, stacked, preferred_element_type=jnp.float32)
        sampled = sampled.reshape(view_count, row_count, 2 * width_cells)
        sampled_density = sampled[:, :, :width_cells]
        sampled_shade = sampled[:, :, width_cells:]
        values = jnp.zeros((view_count, 4, row_count, width_cells), jnp.float32)
        for basis_index in range(basis_count):
            offset = sampled_density * (basis_count - 1) - basis_index
            bump_value = jnp.exp(-0.5 * offset * offset)
            values = values + tf_weights[:, :, basis_index][:, :, None, None] * bump_value[:, None]
        opacity = 1.0 - jnp.exp(-(EXTINCTION / depth_total) * values[:, 3])
        lit_part = sampled_shade * opacity
        emitted = jnp.concatenate([values[:, 0:3] * lit_part[:, None], opacity[:, None]], axis=1)
        colour = colour + passing[:, None] * emitted
        passing = passing * (1.0 - opacity)
        return ((colour, passing), None)

    initial = (
        jnp.zeros((view_count, 4, row_count, width_cells), jnp.float32),
        jnp.ones((view_count, row_count, width_cells), jnp.float32),
    )
    final_state, _ = lax.scan(one_slice, initial, (slab_density, slab_shade))
    return final_state[0].astype(jnp.bfloat16)


def local(density, view_zoom, view_shift, tf_weights, perm_order):
    depth_cells = density.shape[0]
    row_count = density.shape[1]
    width_cells = density.shape[2]
    slab_count = lax.axis_size("depth")
    depth_total = depth_cells * slab_count
    padded = with_halo(density, (("depth", 0), ("tile", 2)), RADIUS)
    shade = occlusion_of(padded, RADIUS, depth_cells, width_cells)
    interp_table = resample_table(view_zoom, view_shift, row_count)
    slab_rgba = render_slab(density, shade, interp_table, tf_weights, depth_total)
    slot_ids = jnp.arange(slab_count, dtype=jnp.int32)
    selector = (perm_order[:, :, None] == slot_ids[None, None, :]).astype(jnp.bfloat16)
    ordered = jnp.einsum(
        "vqj,jvcrx->vqcrx",
        selector,
        lax.all_to_all(slab_rgba[None], "depth", split_axis=3, concat_axis=0, tiled=True),
        preferred_element_type=jnp.float32,
    )
    running = jnp.cumprod(1.0 - ordered[:, :, 3], axis=1)
    leading_ones = jnp.ones_like(running[:, 0:1])
    ahead_pass = jnp.concatenate([leading_ones, running[:, :-1]], axis=1)
    return jnp.sum(ahead_pass[:, :, None] * ordered, axis=1)


def solution(mesh):
    placed = (P("depth", None, "tile"), P(), P(), P(), P())
    return jax.shard_map(
        local, mesh=mesh, in_specs=placed, out_specs=P(None, None, "depth", "tile"), check_vma=False
    )
```

profile of v0, /device:TPU:4, one launch (start us, length us, event | category | flops | bytes accessed | tf_op | source)
XLA Modules:
  0.0 164.9 jit_solution(16466884867182730106)
XLA Ops:
  1.3 3.5 %collective-permute-start = (bf16[8,256,128]{1,2,0:T(8,128)(2,1)S(1)}, bf16[8,256,128]{1,2,0:T(8,128)(2,1)S(1)}, u32[]{:S(2)}, u32[]{:S(2)}) collective-permute-start(bf16[8,256,128]{1,2,0:T(8,128)(2,1)S(1)} %copy.51), channel_id=1, source_target_pairs={{0,8},{8,16},{16,24},{1,9},{9,17},{17,25},{2,10},{10,18},{18,26},{... | collective-permute-start | bytes 1572872 | tf_op jit(solution)/shard_map/ppermute | solution.py:18
  8.9 7.0 %collective-permute-done = bf16[8,256,128]{1,2,0:T(8,128)(2,1)S(1)} collective-permute-done((bf16[8,256,128]{1,2,0:T(8,128)(2,1)S(1)}, bf16[8,256,128]{1,2,0:T(8,128)(2,1)S(1)}, u32[]{:S(2)}, u32[]{:S(2)}) %collective-permute-start) | collective-permute-done | bytes 524320 | tf_op jit(solution)/shard_map/ppermute | solution.py:18
  15.9 4.1 %collective-permute-done.1 = bf16[8,256,128]{1,2,0:T(8,128)(2,1)S(1)} collective-permute-done((bf16[8,256,128]{1,2,0:T(8,128)(2,1)S(1)}, bf16[8,256,128]{1,2,0:T(8,128)(2,1)S(1)}, u32[]{:S(2)}, u32[]{:S(2)}) %collective-permute-start.1) | collective-permute-done | bytes 524320 | tf_op jit(solution)/shard_map/ppermute | solution.py:21
  20.1 1.9 %collective-permute-start.2 = (bf16[24,256,8]{1,2,0:T(8,128)(2,1)S(1)}, bf16[24,256,8]{1,2,0:T(8,128)(2,1)S(1)}, u32[]{:S(2)}, u32[]{:S(2)}) collective-permute-start(bf16[24,256,8]{1,2,0:T(8,128)(2,1)S(1)} %get-tuple-element.190), channel_id=1, source_target_pairs={{0,1},{1,2},{2,3},{3,4},{4,5},{5,6},{6,7},{8,9},{9,10},{10,11},{11... | collective-permute-start | bytes 294920 | tf_op jit(solution)/shard_map/ppermute | solution.py:18
  22.0 4.5 %collective-permute-start.3 = (bf16[24,256,8]{1,2,0:T(8,128)(2,1)S(1)}, bf16[24,256,8]{1,2,0:T(8,128)(2,1)S(1)}, u32[]{:S(2)}, u32[]{:S(2)}) collective-permute-start(bf16[24,256,8]{1,2,0:T(8,128)(2,1)S(1)} %get-tuple-element.191), channel_id=1, source_target_pairs={{1,0},{2,1},{3,2},{4,3},{5,4},{6,5},{7,6},{9,8},{10,9},{11,10},{12... | collective-permute-start | bytes 294920 | tf_op jit(solution)/shard_map/ppermute | solution.py:21
  27.3 1.5 collective-permute-done.3
  28.9 12.5 %multiply_add_fusion.1 = f32[8,256,144]{1,2,0:T(8,128)S(1)} fusion(bf16[24,256,144]{1,2,0:T(8,128)(2,1)S(1)} %pad_maximum_fusion, f32[]{:T(128)} %bitcast.18, f32[]{:T(128)} %bitcast.17, f32[]{:T(128)} %bitcast.16, f32[]{:T(128)} %bitcast.15, f32[]{:T(128)} %bitcast.14, f32[]{:T(128)} %bitcast.13, f32[]{:T(128)} %bitcast.12, f32[]{:T(128)} %bitcast.11, ...), kind=kLoop, calls=%fused_computation.98 | loop fusion | flops 14745600 | bytes 11206724 | tf_op jit(solution)/shard_map/add | solution.py:38
  41.4 15.6 %fusion.38 = f32[8,256,144]{1,2,0:T(8,128)S(1)} fusion(f32[8,256,144]{1,2,0:T(8,128)S(1)} %multiply_add_fusion.1, f32[]{:T(128)} %bitcast.18, f32[]{:T(128)} %bitcast.17, f32[]{:T(128)} %bitcast.16, f32[]{:T(128)} %bitcast.15, f32[]{:T(128)} %bitcast.14, f32[]{:T(128)} %bitcast.13, f32[]{:T(128)} %bitcast.12, f32[]{:T(128)} %bitcast.11, f32[]{:T(128)} %bitcast.10, ...), kind=kLoop, calls=%fused_computation.82 | loop fusion | flops 9732096 | bytes 2359364 | tf_op jit(solution)/shard_map/add | solution.py:45
  56.9 12.8 %fusion.57 = bf16[8,256,128]{1,2,0:T(8,128)(2,1)S(1)} fusion(f32[8,256,144]{1,2,0:T(8,128)S(1)} %fusion.38, f32[]{:T(128)} %bitcast.18, f32[]{:T(128)} %bitcast.17, f32[]{:T(128)} %bitcast.16, f32[]{:T(128)} %bitcast.15, f32[]{:T(128)} %bitcast.14, f32[]{:T(128)} %bitcast.13, f32[]{:T(128)} %bitcast.12, f32[]{:T(128)} %bitcast.11, f32[]{:T(128)} %bitcast.10, ...), kind=kLoop, calls=%fused_computation.103 | loop fusion | flops 9175040 | bytes 18350148 | tf_op jit(solution)/shard_map/convert_element_type | solution.py:53
  69.7 72.9 %while.15 = (s32[]{:T(128)}, f32[2,4,256,128]{3,2,0,1:T(8,128)S(1)}, f32[2,256,128]{2,1,0:T(8,128)}, f32[2,4,8]{1,0,2:T(2,128)S(1)}, bf16[8,256,128]{2,1,0:T(8,1...) while((s32[]{:T(128)}, ...), condition=%wide.region_2.3_spmd.clone, body=%wide.region_1.2_spmd.clone.sunk | while | flops 75300864 | bytes 19140008 | solution.py:94
  72.1 1.3 multiply_exponential_fusion.2
  74.1 1.9 %multiply_add_fusion.3 = f32[2,4,256,128]{3,2,0,1:T(8,128)S(1)} fusion(f32[2,256,128]{2,1,0:T(8,128)} %get-tuple-element.271, f32[2,4]{0,1:T(4,128)S(1)} %copy.83, f32[2,256,128]{2,1,0:T(8,128)} %get-tuple-element.273, f32[2,4]{0,1:T(4,128)S(1)} %copy.84, f32[2,256,128]{2,1,0:T(8,128)} %get-tuple-element.275, f32[2,4]{0,1:T(4,128)S(1)} %copy.85, ...), kind=kLoop, calls=%fused_computation.4.clone.1 | loop fusion | flops 3932160 | bytes 3145984 | tf_op jit(solution)/shard_map/while/body/eval_jaxpr/add | solution.py:82
  80.4 1.3 multiply_exponential_fusion.2
  82.4 1.9 %multiply_add_fusion.3 = f32[2,4,256,128]{3,2,0,1:T(8,128)S(1)} fusion(f32[2,256,128]{2,1,0:T(8,128)} %get-tuple-element.271, f32[2,4]{0,1:T(4,128)S(1)} %copy.83, f32[2,256,128]{2,1,0:T(8,128)} %get-tuple-element.273, f32[2,4]{0,1:T(4,128)S(1)} %copy.84, f32[2,256,128]{2,1,0:T(8,128)} %get-tuple-element.275, f32[2,4]{0,1:T(4,128)S(1)} %copy.85, ...), kind=kLoop, calls=%fused_computation.4.clone.1 | loop fusion | flops 3932160 | bytes 3145984 | tf_op jit(solution)/shard_map/while/body/eval_jaxpr/add | solution.py:82
  84.4 1.7 %fusion.90 = (f32[2,256,128]{2,1,0:T(8,128)}, f32[2,256,128]{2,1,0:T(8,128)S(1)}, f32[2,256,128]{2,1,0:T(8,128)S(1)}) fusion(f32[2,4,256,128]{3,2,0,1:T(8,128)S(1)} %multiply_add_fusion.3, f32[2,256,128]{2,1,0:T(8,128)} %get-tuple-element.301, pred[]{:T(512)S(6)} %compare.5, f32[2,256,256]{2,1,0:T(8,128)S(1)} %bitcast.77), kind=kLoop, calls=%fused_computation.26.clone.1 | loop fusion | flops 393216 | bytes 1572865 | tf_op jit(solution)/shard_map/while/body/eval_jaxpr/mul | solution.py:87
  91.7 1.9 %multiply_add_fusion.3 = f32[2,4,256,128]{3,2,0,1:T(8,128)S(1)} fusion(f32[2,256,128]{2,1,0:T(8,128)} %get-tuple-element.271, f32[2,4]{0,1:T(4,128)S(1)} %copy.83, f32[2,256,128]{2,1,0:T(8,128)} %get-tuple-element.273, f32[2,4]{0,1:T(4,128)S(1)} %copy.84, f32[2,256,128]{2,1,0:T(8,128)} %get-tuple-element.275, f32[2,4]{0,1:T(4,128)S(1)} %copy.85, ...), kind=kLoop, calls=%fused_computation.4.clone.1 | loop fusion | flops 3932160 | bytes 3145984 | tf_op jit(solution)/shard_map/while/body/eval_jaxpr/add | solution.py:82
  93.6 1.7 %fusion.90 = (f32[2,256,128]{2,1,0:T(8,128)}, f32[2,256,128]{2,1,0:T(8,128)S(1)}, f32[2,256,128]{2,1,0:T(8,128)S(1)}) fusion(f32[2,4,256,128]{3,2,0,1:T(8,128)S(1)} %multiply_add_fusion.3, f32[2,256,128]{2,1,0:T(8,128)} %get-tuple-element.301, pred[]{:T(512)S(6)} %compare.5, f32[2,256,256]{2,1,0:T(8,128)S(1)} %bitcast.77), kind=kLoop, calls=%fused_computation.26.clone.1 | loop fusion | flops 393216 | bytes 1572865 | tf_op jit(solution)/shard_map/while/body/eval_jaxpr/mul | solution.py:87
  98.8 1.3 multiply_exponential_fusion.2
  100.9 1.9 %multiply_add_fusion.3 = f32[2,4,256,128]{3,2,0,1:T(8,128)S(1)} fusion(f32[2,256,128]{2,1,0:T(8,128)} %get-tuple-element.271, f32[2,4]{0,1:T(4,128)S(1)} %copy.83, f32[2,256,128]{2,1,0:T(8,128)} %get-tuple-element.273, f32[2,4]{0,1:T(4,128)S(1)} %copy.84, f32[2,256,128]{2,1,0:T(8,128)} %get-tuple-element.275, f32[2,4]{0,1:T(4,128)S(1)} %copy.85, ...), kind=kLoop, calls=%fused_computation.4.clone.1 | loop fusion | flops 3932160 | bytes 3145984 | tf_op jit(solution)/shard_map/while/body/eval_jaxpr/add | solution.py:82
  102.8 1.7 %fusion.90 = (f32[2,256,128]{2,1,0:T(8,128)}, f32[2,256,128]{2,1,0:T(8,128)S(1)}, f32[2,256,128]{2,1,0:T(8,128)S(1)}) fusion(f32[2,4,256,128]{3,2,0,1:T(8,128)S(1)} %multiply_add_fusion.3, f32[2,256,128]{2,1,0:T(8,128)} %get-tuple-element.301, pred[]{:T(512)S(6)} %compare.5, f32[2,256,256]{2,1,0:T(8,128)S(1)} %bitcast.77), kind=kLoop, calls=%fused_computation.26.clone.1 | loop fusion | flops 393216 | bytes 1572865 | tf_op jit(solution)/shard_map/while/body/eval_jaxpr/mul | solution.py:87
  108.1 1.3 multiply_exponential_fusion.2
  110.1 1.9 %multiply_add_fusion.3 = f32[2,4,256,128]{3,2,0,1:T(8,128)S(1)} fusion(f32[2,256,128]{2,1,0:T(8,128)} %get-tuple-element.271, f32[2,4]{0,1:T(4,128)S(1)} %copy.83, f32[2,256,128]{2,1,0:T(8,128)} %get-tuple-element.273, f32[2,4]{0,1:T(4,128)S(1)} %copy.84, f32[2,256,128]{2,1,0:T(8,128)} %get-tuple-element.275, f32[2,4]{0,1:T(4,128)S(1)} %copy.85, ...), kind=kLoop, calls=%fused_computation.4.clone.1 | loop fusion | flops 3932160 | bytes 3145984 | tf_op jit(solution)/shard_map/while/body/eval_jaxpr/add | solution.py:82
  112.0 1.7 %fusion.90 = (f32[2,256,128]{2,1,0:T(8,128)}, f32[2,256,128]{2,1,0:T(8,128)S(1)}, f32[2,256,128]{2,1,0:T(8,128)S(1)}) fusion(f32[2,4,256,128]{3,2,0,1:T(8,128)S(1)} %multiply_add_fusion.3, f32[2,256,128]{2,1,0:T(8,128)} %get-tuple-element.301, pred[]{:T(512)S(6)} %compare.5, f32[2,256,256]{2,1,0:T(8,128)S(1)} %bitcast.77), kind=kLoop, calls=%fused_computation.26.clone.1 | loop fusion | flops 393216 | bytes 1572865 | tf_op jit(solution)/shard_map/while/body/eval_jaxpr/mul | solution.py:87
  119.3 1.9 %multiply_add_fusion.3 = f32[2,4,256,128]{3,2,0,1:T(8,128)S(1)} fusion(f32[2,256,128]{2,1,0:T(8,128)} %get-tuple-element.271, f32[2,4]{0,1:T(4,128)S(1)} %copy.83, f32[2,256,128]{2,1,0:T(8,128)} %get-tuple-element.273, f32[2,4]{0,1:T(4,128)S(1)} %copy.84, f32[2,256,128]{2,1,0:T(8,128)} %get-tuple-element.275, f32[2,4]{0,1:T(4,128)S(1)} %copy.85, ...), kind=kLoop, calls=%fused_computation.4.clone.1 | loop fusion | flops 3932160 | bytes 3145984 | tf_op jit(solution)/shard_map/while/body/eval_jaxpr/add | solution.py:82
  121.3 1.7 %fusion.90 = (f32[2,256,128]{2,1,0:T(8,128)}, f32[2,256,128]{2,1,0:T(8,128)S(1)}, f32[2,256,128]{2,1,0:T(8,128)S(1)}) fusion(f32[2,4,256,128]{3,2,0,1:T(8,128)S(1)} %multiply_add_fusion.3, f32[2,256,128]{2,1,0:T(8,128)} %get-tuple-element.301, pred[]{:T(512)S(6)} %compare.5, f32[2,256,256]{2,1,0:T(8,128)S(1)} %bitcast.77), kind=kLoop, calls=%fused_computation.26.clone.1 | loop fusion | flops 393216 | bytes 1572865 | tf_op jit(solution)/shard_map/while/body/eval_jaxpr/mul | solution.py:87
  126.5 1.3 multiply_exponential_fusion.2
  128.6 1.9 %multiply_add_fusion.3 = f32[2,4,256,128]{3,2,0,1:T(8,128)S(1)} fusion(f32[2,256,128]{2,1,0:T(8,128)} %get-tuple-element.271, f32[2,4]{0,1:T(4,128)S(1)} %copy.83, f32[2,256,128]{2,1,0:T(8,128)} %get-tuple-element.273, f32[2,4]{0,1:T(4,128)S(1)} %copy.84, f32[2,256,128]{2,1,0:T(8,128)} %get-tuple-element.275, f32[2,4]{0,1:T(4,128)S(1)} %copy.85, ...), kind=kLoop, calls=%fused_computation.4.clone.1 | loop fusion | flops 3932160 | bytes 3145984 | tf_op jit(solution)/shard_map/while/body/eval_jaxpr/add | solution.py:82
  130.5 1.7 %fusion.90 = (f32[2,256,128]{2,1,0:T(8,128)}, f32[2,256,128]{2,1,0:T(8,128)S(1)}, f32[2,256,128]{2,1,0:T(8,128)S(1)}) fusion(f32[2,4,256,128]{3,2,0,1:T(8,128)S(1)} %multiply_add_fusion.3, f32[2,256,128]{2,1,0:T(8,128)} %get-tuple-element.301, pred[]{:T(512)S(6)} %compare.5, f32[2,256,256]{2,1,0:T(8,128)S(1)} %bitcast.77), kind=kLoop, calls=%fused_computation.26.clone.1 | loop fusion | flops 393216 | bytes 1572865 | tf_op jit(solution)/shard_map/while/body/eval_jaxpr/mul | solution.py:87
  137.8 1.9 %multiply_add_fusion.3 = f32[2,4,256,128]{3,2,0,1:T(8,128)S(1)} fusion(f32[2,256,128]{2,1,0:T(8,128)} %get-tuple-element.271, f32[2,4]{0,1:T(4,128)S(1)} %copy.83, f32[2,256,128]{2,1,0:T(8,128)} %get-tuple-element.273, f32[2,4]{0,1:T(4,128)S(1)} %copy.84, f32[2,256,128]{2,1,0:T(8,128)} %get-tuple-element.275, f32[2,4]{0,1:T(4,128)S(1)} %copy.85, ...), kind=kLoop, calls=%fused_computation.4.clone.1 | loop fusion | flops 3932160 | bytes 3145984 | tf_op jit(solution)/shard_map/while/body/eval_jaxpr/add | solution.py:82
  139.7 1.7 %fusion.90 = (f32[2,256,128]{2,1,0:T(8,128)}, f32[2,256,128]{2,1,0:T(8,128)S(1)}, f32[2,256,128]{2,1,0:T(8,128)S(1)}) fusion(f32[2,4,256,128]{3,2,0,1:T(8,128)S(1)} %multiply_add_fusion.3, f32[2,256,128]{2,1,0:T(8,128)} %get-tuple-element.301, pred[]{:T(512)S(6)} %compare.5, f32[2,256,256]{2,1,0:T(8,128)S(1)} %bitcast.77), kind=kLoop, calls=%fused_computation.26.clone.1 | loop fusion | flops 393216 | bytes 1572865 | tf_op jit(solution)/shard_map/while/body/eval_jaxpr/mul | solution.py:87
  143.1 19.1 %all_to_all.18 = bf16[1,2,4,256,128]{4,2,1,0,3:T(4,128)(2,1)S(1)} all-to-all(bf16[1,2,4,256,128]{4,2,1,0,3:T(4,128)(2,1)S(1)} %bitcast.78), channel_id=1, replica_groups=mesh['depth'=4,'tile'=8] {'depth'}, dimensions={3} | all-to-all | bytes 1048576 | tf_op jit(solution)/shard_map/all_to_all | solution.py:113
  163.5 1.4 multiply_reduce_fusion
  (193 shorter events, 46.2 us)
Async XLA Ops:
  1.3 14.7 %collective-permute-start = (bf16[8,256,128]{1,2,0:T(8,128)(2,1)S(1)}, bf16[8,256,128]{1,2,0:T(8,128)(2,1)S(1)}, u32[]{:S(2)}, u32[]{:S(2)}) collective-permute-start(bf16[8,256,128]{1,2,0:T(8,128)(2,1)S(1)} %copy.51), channel_id=1, source_target_pairs={{0,8},{8,16},{16,24},{1,9},{9,17},{17,25},{2,10},{10,18},{18,26},{... | collective-permute-start | bytes 1572872 | tf_op jit(solution)/shard_map/ppermute | solution.py:18
  4.8 15.3 %collective-permute-start.1 = (bf16[8,256,128]{1,2,0:T(8,128)(2,1)S(1)}, bf16[8,256,128]{1,2,0:T(8,128)(2,1)S(1)}, u32[]{:S(2)}, u32[]{:S(2)}) collective-permute-start(bf16[8,256,128]{1,2,0:T(8,128)(2,1)S(1)} %copy.51), channel_id=1, source_target_pairs={{8,0},{16,8},{24,16},{9,1},{17,9},{25,17},{10,2},{18,10},{26,18},{... | collective-permute-start | bytes 1572872 | tf_op jit(solution)/shard_map/ppermute | solution.py:21
  20.1 7.2 %collective-permute-start.2 = (bf16[24,256,8]{1,2,0:T(8,128)(2,1)S(1)}, bf16[24,256,8]{1,2,0:T(8,128)(2,1)S(1)}, u32[]{:S(2)}, u32[]{:S(2)}) collective-permute-start(bf16[24,256,8]{1,2,0:T(8,128)(2,1)S(1)} %get-tuple-element.190), channel_id=1, source_target_pairs={{0,1},{1,2},{2,3},{3,4},{4,5},{5,6},{6,7},{8,9},{9,10},{10,11},{11... | collective-permute-start | bytes 294920 | tf_op jit(solution)/shard_map/ppermute | solution.py:18
  22.0 6.7 %collective-permute-start.3 = (bf16[24,256,8]{1,2,0:T(8,128)(2,1)S(1)}, bf16[24,256,8]{1,2,0:T(8,128)(2,1)S(1)}, u32[]{:S(2)}, u32[]{:S(2)}) collective-permute-start(bf16[24,256,8]{1,2,0:T(8,128)(2,1)S(1)} %get-tuple-element.191), channel_id=1, source_target_pairs={{1,0},{2,1},{3,2},{4,3},{5,4},{6,5},{7,6},{9,8},{10,9},{11,10},{12... | collective-permute-start | bytes 294920 | tf_op jit(solution)/shard_map/ppermute | solution.py:21
  69.7 0.8 copy-start
  77.0 1.0 copy-start.1
  78.0 0.8 copy-start
  86.2 1.0 copy-start.1
  87.3 0.8 copy-start
  95.4 1.0 copy-start.1
  96.5 0.8 copy-start
  104.7 1.0 copy-start.1
  105.7 0.8 copy-start
  113.9 1.0 copy-start.1
  114.9 0.8 copy-start
  123.1 1.0 copy-start.1
  124.2 0.8 copy-start
  132.4 1.0 copy-start.1
  133.4 0.8 copy-start
  141.6 1.0 copy-start.1
  142.7 19.5 %copy-start.2 = (s32[2,4]{1,0:T(2,128)S(1)}, s32[2,4]{1,0:T(2,128)}, u32[]{:S(2)}) copy-start(s32[2,4]{1,0:T(2,128)} %param.11) | copy-start | bytes 100
where the time goes:
time: 167 us; the launch traced here: 165 us
  other arithmetic  87.5 us (52%)
  local copies, waits for them, and re-layouts  30 us (18%)
  blocking collectives  19.1 us (11%)
  waiting for transfers between devices  12.6 us (8%)
  starting transfers between devices  11.3 us (7%)
  matrix products  3.66 us (2%)
    all_to_all x1, blocking collectives, local(): lax.all_to_all(slab_rgba[None], 'depth', split_axis=3, concat_axis=0, til...  19.1 us
    add x1, other arithmetic, occlusion_of(): along_rows + tap_weights[tap_index] * padded_rows[:, tap_index:tap_index...  15.6 us
    add x8, other arithmetic, one_slice(): values + tf_weights[:, :, basis_index][:, :, None, None] * bump_value[:,...  15.3 us
    mul x8, other arithmetic, one_slice(): passing = passing * (1.0 - opacity)  13 us
    convert_element_type x1, other arithmetic, occlusion_of(): return jnp.exp(-OCCLUSION_GAIN * along_width).astype(jnp.bfloat16)  12.8 us
    add x1, other arithmetic, occlusion_of(): along_depth + tap_weights[tap_index] * padded[tap_index:tap_index + depth...  12.5 us
    while x32, local copies, waits for them, and re-layouts  11.6 us
    exp x8, other arithmetic, one_slice(): bump_value = jnp.exp(-0.5 * offset * offset)  10.5 us
  transfers between devices with their start and end apart: 4, of which 3 were waited for; matrix products, arithmetic and copies ran while one was open for 2% of the time, Pallas kernels for 0%

commit v1 on v0

v1 whole, which is shorter than its diff:
```python
import functools
import math

import jax
import jax.numpy as jnp
import numpy as np
from jax import lax
from jax.experimental import pallas as pl
from jax.experimental.pallas import tpu as pltpu
from jax.sharding import PartitionSpec as P

RADIUS = 8
OCCLUSION_GAIN = 1.5
EXTINCTION = 0.5
LOG2E = math.log2(math.e)
GROUP = 16
CHUNK = 32


def rounded_taps():
    offsets = np.arange(-RADIUS, RADIUS + 1, dtype=np.float64)
    taps = np.exp(-offsets * offsets / 72.0)
    taps = (taps / taps.sum()).astype(jnp.bfloat16).astype(np.float64)
    return taps, float(taps.sum())


def band(out_count, in_count, shift, taps):
    offset = np.arange(in_count)[None, :] + shift - np.arange(out_count)[:, None]
    inside = np.abs(offset) <= RADIUS
    return np.where(inside, taps[np.clip(offset + RADIUS, 0, 2 * RADIUS)], 0.0)


def constants(cells, rows, width):
    taps, total = rounded_taps()
    pack = np.zeros((cells, width, width), np.float32)
    low = np.zeros((width, cells, width))
    high = np.zeros((width, cells, width))
    half = cells * RADIUS
    from_low = band(width, RADIUS, -RADIUS, taps).T
    from_high = band(width, RADIUS, width, taps).T
    for z in range(cells):
        for j in range(RADIUS):
            pack[z, j, z * RADIUS + j] = 1.0
            pack[z, width - RADIUS + j, half + z * RADIUS + j] = 1.0
        low[half + z * RADIUS : half + (z + 1) * RADIUS, z] = from_low
        high[z * RADIUS : (z + 1) * RADIUS, z] = from_high
    halo = np.concatenate([low, high]).reshape(2 * width, cells * width)
    depth = np.kron(band(cells, 3 * cells, -cells, taps), np.eye(GROUP))
    arrays = (
        pack.reshape(cells * width, width),
        band(width, width, 0, taps).T,
        halo,
        band(rows, rows, 0, taps),
        depth,
    )
    return [jnp.asarray(a.astype(jnp.bfloat16)) for a in arrays], total


def matmul(a, b):
    return jnp.dot(a, b, preferred_element_type=jnp.float32)


def kernel(
    slabs, tiles, tap_total,
    density, zoom, shift, weights, order, pack_m, width_m, halo_m, height_m, depth_m,
    image,
    table, packed, from_left, from_right, plane, from_low, from_high, sampled, lit, shade, slab, *rest,
):
    views, channels, basis = weights.shape
    cells, rows, width = density.shape
    recv = rest[:views]
    tile_send, tile_recv, depth_send, depth_recv, slab_send, slab_recv = rest[views:]
    group_rows = rows // slabs
    d = lax.axis_index("depth")
    t = lax.axis_index("tile")
    bf16 = jnp.bfloat16

    barrier = pltpu.get_barrier_semaphore()

    def greet(peer):
        pl.semaphore_signal(barrier, inc=1, device_id=peer, device_id_type=pl.DeviceIdType.MESH)

    for j in range(slabs):
        @pl.when(j != d)
        def _():
            greet({"depth": j})

    @pl.when(t > 0)
    def _():
        greet({"tile": t - 1})

    @pl.when(t < tiles - 1)
    def _():
        greet({"tile": t + 1})

    def remote(src, dst, send, recv_sem, peer):
        return pltpu.make_async_remote_copy(
            src_ref=src, dst_ref=dst, send_sem=send, recv_sem=recv_sem,
            device_id=peer, device_id_type=pl.DeviceIdType.MESH,
        )

    whole = jnp.concatenate([density[z] for z in range(cells)], axis=1)
    packed[...] = matmul(whole, pack_m[...]).astype(bf16)
    to_left = remote(packed, from_right, tile_send.at[0], tile_recv.at[1], {"tile": t - 1})
    to_right = remote(packed, from_left, tile_send.at[1], tile_recv.at[0], {"tile": t + 1})

    pl.semaphore_wait(
        barrier, slabs - 1 + (t > 0).astype(jnp.int32) + (t < tiles - 1).astype(jnp.int32)
    )

    @pl.when(t > 0)
    def _():
        to_left.start()

    @pl.when(t < tiles - 1)
    def _():
        to_right.start()

    @pl.when(t == 0)
    def _():
        from_left[...] = jnp.zeros_like(from_left)

    @pl.when(t == tiles - 1)
    def _():
        from_right[...] = jnp.zeros_like(from_right)

    @pl.when(d == 0)
    def _():
        from_low[...] = jnp.zeros_like(from_low)

    @pl.when(d == slabs - 1)
    def _():
        from_high[...] = jnp.zeros_like(from_high)

    pixel = lax.broadcasted_iota(jnp.int32, (rows, rows), 0).astype(jnp.float32)
    cell = lax.broadcasted_iota(jnp.int32, (rows, rows), 1).astype(jnp.float32)
    for v in range(views):
        where_at = zoom[v] * pixel + shift[v]
        table[v * rows : (v + 1) * rows] = jnp.maximum(0.0, 1.0 - jnp.abs(where_at - cell)).astype(bf16)

    def resample(source):
        for z in range(0, cells, 2):
            pair = matmul(table[...], jnp.concatenate([source[z], source[z + 1]], axis=1))
            sampled[z] = pair[:, :width]
            sampled[z + 1] = pair[:, width:]

    resample(density)
    inner = matmul(density[...].reshape(cells * rows, width), width_m[...])

    @pl.when(t > 0)
    def _():
        to_left.wait_send()
        to_right.wait_recv()

    @pl.when(t < tiles - 1)
    def _():
        to_right.wait_send()
        to_left.wait_recv()

    outer = matmul(jnp.concatenate([from_left[...], from_right[...]], axis=1), halo_m[...])
    along_width = jnp.concatenate(
        [inner[z * rows : (z + 1) * rows] + outer[:, z * width : (z + 1) * width] for z in range(cells)],
        axis=1,
    ).astype(bf16)
    flat = matmul(height_m[...], along_width).astype(bf16)
    for z in range(cells):
        plane[z] = flat[:, z * width : (z + 1) * width]

    to_below = remote(plane, from_high, depth_send.at[0], depth_recv.at[1], {"depth": d - 1})
    to_above = remote(plane, from_low, depth_send.at[1], depth_recv.at[0], {"depth": d + 1})

    @pl.when(d > 0)
    def _():
        to_below.start()

    @pl.when(d < slabs - 1)
    def _():
        to_above.start()

    chunk = min(CHUNK, group_rows)
    per_group = group_rows // chunk
    extinction = -(EXTINCTION / (cells * slabs)) * LOG2E
    peak = basis - 1
    for v in range(views):
        coef = [
            [
                weights[v, c, k] * (math.exp(-0.5 * k * k) * (extinction if c == channels - 1 else 1.0))
                for k in range(basis)
            ]
            for c in range(channels)
        ]

        def transfer(i, carry, v=v, coef=coef):
            first = pl.multiple_of(i * chunk, chunk)
            passing = jnp.ones((chunk, width), jnp.float32)
            for z in range(cells):
                s = sampled[z, pl.ds(v * rows + first, chunk), :]
                fall = jnp.exp2((-0.5 * peak * peak * LOG2E) * (s * s))
                ratio = jnp.exp2((peak * LOG2E) * s)
                sums = []
                for c in range(channels):
                    total = coef[c][basis - 1] * ratio + coef[c][basis - 2]
                    for k in range(basis - 3, -1, -1):
                        total = total * ratio + coef[c][k]
                    sums.append(total)
                later = passing * jnp.exp2(fall * sums[-1])
                share = (passing - later) * fall
                for c in range(channels - 1):
                    lit[v, c, z, pl.ds(first, chunk), :] = share * sums[c]
                passing = later
            group = i // per_group
            inside = pl.multiple_of((i % per_group) * chunk, chunk)
            slab[v, group, channels - 1, pl.ds(inside, chunk), :] = (1.0 - passing).astype(bf16)
            return carry

        lax.fori_loop(0, rows // chunk, transfer, 0)

    @pl.when(d > 0)
    def _():
        to_below.wait_send()
        to_above.wait_recv()

    @pl.when(d < slabs - 1)
    def _():
        to_above.wait_send()
        to_below.wait_recv()

    gain = -OCCLUSION_GAIN * LOG2E / tap_total**3
    for g in range(0, rows, 2 * GROUP):
        def column(at):
            part = pl.ds(at, GROUP)
            return jnp.concatenate(
                [ref[:, part, :].reshape(cells * GROUP, width) for ref in (from_low, plane, from_high)], axis=0
            )

        both = matmul(depth_m[...], jnp.concatenate([column(g), column(g + GROUP)], axis=1))
        both = jnp.exp2(gain * both).astype(bf16)
        shade[:, g : g + GROUP, :] = both[:, :width].reshape(cells, GROUP, width)
        shade[:, g + GROUP : g + 2 * GROUP, :] = both[:, width:].reshape(cells, GROUP, width)
    resample(shade)

    def slab_copy(v, j):
        return remote(slab.at[v, j], recv[v].at[d], slab_send.at[v, j], slab_recv.at[v, d], {"depth": j})

    for v in range(views):
        for j in range(slabs):
            for i in range(per_group):
                here = slice(i * chunk, (i + 1) * chunk)
                at = slice(j * group_rows + i * chunk, j * group_rows + (i + 1) * chunk)
                colour = [jnp.zeros((chunk, width), jnp.float32)] * (channels - 1)
                for z in range(cells):
                    s = sampled[z, v * rows + at.start : v * rows + at.stop, :]
                    colour = [colour[c] + lit[v, c, z, at, :] * s for c in range(channels - 1)]
                for c in range(channels - 1):
                    slab[v, j, c, here, :] = colour[c].astype(bf16)

            @pl.when(j != d)
            def _():
                slab_copy(v, j).start()

            @pl.when(j == d)
            def _():
                recv[v][d] = slab[v, j]

    for v in range(views):
        for j in range(slabs):
            @pl.when(j != d)
            def _():
                slab_copy(v, j).wait_send()
                remote(slab.at[v, j], recv[v].at[j], slab_send.at[v, j], slab_recv.at[v, j], {"depth": j}).wait_recv()

        picture = jnp.zeros((channels, group_rows, width), jnp.float32)
        passing = jnp.ones((group_rows, width), jnp.float32)
        for q in range(slabs):
            layer = recv[v][order[v, q]].astype(jnp.float32)
            picture = picture + passing[None] * layer
            passing = passing * (1.0 - layer[channels - 1])
        image[v] = picture


def local(slabs, tiles, density, view_zoom, view_shift, tf_weights, perm_order):
    cells, rows, width = density.shape
    views, channels, _ = tf_weights.shape
    group_rows = rows // slabs
    matrices, tap_total = constants(cells, rows, width)
    vmem = pl.BlockSpec(memory_space=pltpu.VMEM)
    smem = pl.BlockSpec(memory_space=pltpu.SMEM)
    bf16 = jnp.bfloat16
    block = pltpu.VMEM((cells, rows, width), bf16)
    edge = pltpu.VMEM((rows, width), bf16)
    dma = pltpu.SemaphoreType.DMA
    return pl.pallas_call(
        functools.partial(kernel, slabs, tiles, tap_total),
        out_shape=jax.ShapeDtypeStruct((views, channels, group_rows, width), jnp.float32),
        in_specs=[vmem, smem, smem, smem, smem] + [vmem] * len(matrices),
        out_specs=vmem,
        scratch_shapes=[
            pltpu.VMEM((views * rows, rows), bf16),
            edge, edge, edge,
            block, block, block,
            pltpu.VMEM((cells, views * rows, width), jnp.float32),
            pltpu.VMEM((views, channels - 1, cells, rows, width), jnp.float32),
            block,
            pltpu.VMEM((views, slabs, channels, group_rows, width), bf16),
        ]
        + [pltpu.VMEM((slabs, channels, group_rows, width), bf16)] * views
        + [dma((2,)), dma((2,)), dma((2,)), dma((2,)), dma((views, slabs)), dma((views, slabs))],
        compiler_params=pltpu.CompilerParams(
            collective_id=0, has_side_effects=True, vmem_limit_bytes=60 * 1024 * 1024
        ),
    )(density, view_zoom, view_shift, tf_weights, perm_order, *matrices)


def solution(mesh):
    placed = (P("depth", None, "tile"), P(), P(), P(), P())
    return jax.shard_map(
        functools.partial(local, mesh.shape["depth"], mesh.shape["tile"]),
        mesh=mesh, in_specs=placed, out_specs=P(None, None, "depth", "tile"), check_vma=False,
    )
```

time: 167 us -> 37.6 us (0.23); the launches traced: 165 us -> 37.5 us
  other arithmetic: 87.5 us -> 0 us
  Pallas kernels: 0 us -> 35.8 us
  local copies, waits for them, and re-layouts: 30 us -> 1.67 us
  blocking collectives: 19.1 us -> 0 us
  waiting for transfers between devices: 12.6 us -> 0 us
  starting transfers between devices: 11.3 us -> 0 us
  matrix products: 3.66 us -> 0 us
    add x18 -> x0, other arithmetic: 46.4 us -> none  [the longest x1 15.6 us: occlusion_of(): along_rows + tap_weights[tap_index] * padded_rows[:, tap_index:tap_index...]
    pallas_call x0 -> x1, Pallas kernels: none -> 35.8 us  [local(): pl.pallas_call(functools.partial(kernel, slabs, tiles, tap_total), out_sh...]
    all_to_all x1 -> x0, blocking collectives: 19.1 us -> none  [local(): lax.all_to_all(slab_rgba[None], 'depth', split_axis=3, concat_axis=0, til...]
    mul x16 -> x0, other arithmetic: 13.5 us -> none  [the longest x8 13 us: one_slice(): passing = passing * (1.0 - opacity)]
    convert_element_type x2 -> x0, other arithmetic: 12.9 us -> none  [the longest x1 12.8 us: occlusion_of(): return jnp.exp(-OCCLUSION_GAIN * along_width).astype(jnp.bfloat16)]
    ppermute x4 -> x0, waiting for transfers between devices: 12.6 us -> none  [the longest x2 7.03 us: with_halo(): lax.ppermute(lax.slice_in_dim(block, block.shape[dim] - width, None, axis...]
    while x32 -> x0, local copies, waits for them, and re-layouts: 11.6 us -> none
    ppermute x4 -> x0, starting transfers between devices: 11.3 us -> none  [the longest x2 5.83 us: with_halo(): lax.ppermute(lax.slice_in_dim(block, 0, width, axis=dim), axis, backward)]
  transfers between devices with their start and end apart: 4 -> 0, of which waited for: 3 -> 0; matrix products, arithmetic and copies ran while one was open for 2% -> 0% of each run, Pallas kernels for 0% -> 0%
where the time goes in v1:
time: 37.6 us; the launch traced here: 37.5 us
  Pallas kernels  35.8 us (95%)
  local copies, waits for them, and re-layouts  1.67 us (4%)
    pallas_call x1, Pallas kernels, local(): pl.pallas_call(functools.partial(kernel, slabs, tiles, tap_total), out_sh...  35.8 us
    unnamed x1, local copies, waits for them, and re-layouts  1.67 us

profile of v1, /device:TPU:4, one launch (start us, length us, event | category | flops | bytes accessed | tf_op | source)
XLA Modules:
  0.0 37.5 jit_solution(6260675212822613253)
XLA Ops:
  0.0 35.8 %shard_map.100 = f32[2,4,64,128]{3,2,1,0:T(8,128)} custom-call(bf16[8,256,128]{2,1,0:T(8,128)(2,1)} %density.1, f32[2]{0:T(128)} %zoom.1, f32[2]{0:T(128)} %shift.1, f32[2,4,8]{2,1,0:T(4,128)} %weights.1, s32[2,4]{1,0:T(2,128)} %order.1, bf16[1024,128]{1,0:T(8,128)(2,1)} %constant.10.clone.pack_m, bf16[128,128]{1,0:T(8,128)(2,1)} %constant.11.clone.width_m, ...), custom_call_target="tpu_custom_call" | custom-call | tf_op jit(solution)/shard_map/pallas_call | solution.py:292
  35.8 1.7 %copy.12 = f32[2,4,64,128]{3,2,1,0:T(8,128)} copy(f32[2,4,64,128]{3,2,1,0:T(8,128)} %shard_map.100) | data formatting | bytes 524288

commit v2 on v1

--- a/solution.py
+++ b/solution.py
@@ -12,6 +12,8 @@
 RADIUS = 8
 OCCLUSION_GAIN = 1.5
 EXTINCTION = 0.5
+MAX_ZOOM = 0.9
+MAX_SHIFT = 16.0
 LOG2E = math.log2(math.e)
 GROUP = 16
 CHUNK = 32
@@ -62,14 +64,16 @@
 
 def kernel(
     slabs, tiles, tap_total,
-    density, zoom, shift, weights, order, pack_m, width_m, halo_m, height_m, depth_m,
+    density_in, zoom, shift, weights, order, pack_in, width_in, halo_in, height_in, depth_in,
     image,
-    table, packed, from_left, from_right, plane, from_low, from_high, sampled, lit, shade, slab, *rest,
+    density, pack_m, width_m, halo_m, height_m, depth_m,
+    table, packed, from_left, from_right, plane, from_low, from_high, sampled, lit, shade, alpha, slab, recv_alpha, *rest,
 ):
     views, channels, basis = weights.shape
-    cells, rows, width = density.shape
+    cells, rows, width = density_in.shape
+    used = used_rows(rows)
     recv = rest[:views]
-    tile_send, tile_recv, depth_send, depth_recv, slab_send, slab_recv = rest[views:]
+    fetch_sem, tile_send, tile_recv, depth_send, depth_recv, alpha_send, alpha_recv, slab_send, slab_recv = rest[views:]
     group_rows = rows // slabs
     d = lax.axis_index("depth")
     t = lax.axis_index("tile")
@@ -92,6 +96,16 @@
     @pl.when(t < tiles - 1)
     def _():
         greet({"tile": t + 1})
+
+    sources = (density_in, pack_in, width_in, halo_in, height_in, depth_in)
+    places = (density, pack_m, width_m, halo_m, height_m, depth_m)
+    fetches = [
+        pltpu.make_async_copy(src, dst, fetch_sem.at[i]) for i, (src, dst) in enumerate(zip(sources, places))
+    ]
+    for fetch in fetches:
+        fetch.start()
+    fetches[0].wait()
+    fetches[1].wait()
 
     def remote(src, dst, send, recv_sem, peer):
         return pltpu.make_async_remote_copy(
@@ -124,6 +138,10 @@
     def _():
         from_right[...] = jnp.zeros_like(from_right)
 
+    if used < rows:
+        from_low[:, used:] = jnp.zeros((cells, rows - used, width), bf16)
+        from_high[:, used:] = jnp.zeros((cells, rows - used, width), bf16)
+
     @pl.when(d == 0)
     def _():
         from_low[...] = jnp.zeros_like(from_low)
@@ -145,6 +163,8 @@
             sampled[z + 1] = pair[:, width:]
 
     resample(density)
+    for fetch in fetches[2:]:
+        fetch.wait()
     inner = matmul(density[...].reshape(cells * rows, width), width_m[...])
 
     @pl.when(t > 0)
@@ -166,8 +186,8 @@
     for z in range(cells):
         plane[z] = flat[:, z * width : (z + 1) * width]
 
-    to_below = remote(plane, from_high, depth_send.at[0], depth_recv.at[1], {"depth": d - 1})
-    to_above = remote(plane, from_low, depth_send.at[1], depth_recv.at[0], {"depth": d + 1})
+    to_below = remote(plane.at[:, :used], from_high.at[:, :used], depth_send.at[0], depth_recv.at[1], {"depth": d - 1})
+    to_above = remote(plane.at[:, :used], from_low.at[:, :used], depth_send.at[1], depth_recv.at[0], {"depth": d + 1})
 
     @pl.when(d > 0)
     def _():
@@ -210,7 +230,7 @@
                 passing = later
             group = i // per_group
             inside = pl.multiple_of((i % per_group) * chunk, chunk)
-            slab[v, group, channels - 1, pl.ds(inside, chunk), :] = (1.0 - passing).astype(bf16)
+            alpha[group, v, pl.ds(inside, chunk), :] = (1.0 - passing).astype(bf16)
             return carry
 
         lax.fori_loop(0, rows // chunk, transfer, 0)
@@ -224,6 +244,17 @@
     def _():
         to_above.wait_send()
         to_below.wait_recv()
+
+    def peer_of(k):
+        return lax.rem(d + k, slabs)
+
+    def alpha_copy(k):
+        return remote(alpha.at[peer_of(k)], recv_alpha.at[d], alpha_send.at[k], alpha_recv.at[d], {"depth": peer_of(k)})
+
+    others = sorted(range(1, slabs), key=lambda k: abs(2 * k - slabs))
+    for k in others:
+        alpha_copy(k).start()
+    recv_alpha[d] = alpha[d]
 
     gain = -OCCLUSION_GAIN * LOG2E / tap_total**3
     for g in range(0, rows, 2 * GROUP):
@@ -239,43 +270,61 @@
         shade[:, g + GROUP : g + 2 * GROUP, :] = both[:, width:].reshape(cells, GROUP, width)
     resample(shade)
 
-    def slab_copy(v, j):
-        return remote(slab.at[v, j], recv[v].at[d], slab_send.at[v, j], slab_recv.at[v, d], {"depth": j})
+    def slab_copy(v, k):
+        return remote(
+            slab.at[v, k], recv[v].at[d], slab_send.at[v, k], slab_recv.at[v, d], {"depth": peer_of(k)}
+        )
 
     for v in range(views):
-        for j in range(slabs):
+        for k in others + [0]:
+            start = pl.multiple_of(peer_of(k) * group_rows, group_rows)
             for i in range(per_group):
-                here = slice(i * chunk, (i + 1) * chunk)
-                at = slice(j * group_rows + i * chunk, j * group_rows + (i + 1) * chunk)
                 colour = [jnp.zeros((chunk, width), jnp.float32)] * (channels - 1)
                 for z in range(cells):
-                    s = sampled[z, v * rows + at.start : v * rows + at.stop, :]
-                    colour = [colour[c] + lit[v, c, z, at, :] * s for c in range(channels - 1)]
+                    s = sampled[z, pl.ds(v * rows + start + i * chunk, chunk), :]
+                    colour = [
+                        colour[c] + lit[v, c, z, pl.ds(start + i * chunk, chunk), :] * s
+                        for c in range(channels - 1)
+                    ]
                 for c in range(channels - 1):
-                    slab[v, j, c, here, :] = colour[c].astype(bf16)
-
-            @pl.when(j != d)
-            def _():
-                slab_copy(v, j).start()
-
-            @pl.when(j == d)
-            def _():
-                recv[v][d] = slab[v, j]
-
+                    tint = colour[c].astype(bf16)
+                    if k:
+                        slab[v, k, c, i * chunk : (i + 1) * chunk, :] = tint
+                    else:
+                        recv[v][d, c, i * chunk : (i + 1) * chunk, :] = tint
+            if k:
+                slab_copy(v, k).start()
+
+    for k in others:
+        peer = peer_of(k)
+        alpha_copy(k).wait_send()
+        remote(
+            alpha.at[peer], recv_alpha.at[peer], alpha_send.at[k], alpha_recv.at[peer], {"depth": peer}
+        ).wait_recv()
     for v in range(views):
-        for j in range(slabs):
-            @pl.when(j != d)
-            def _():
-                slab_copy(v, j).wait_send()
-                remote(slab.at[v, j], recv[v].at[j], slab_send.at[v, j], slab_recv.at[v, j], {"depth": j}).wait_recv()
-
-        picture = jnp.zeros((channels, group_rows, width), jnp.float32)
+        for k in others:
+            peer = peer_of(k)
+            slab_copy(v, k).wait_send()
+            remote(
+                slab.at[v, k], recv[v].at[peer], slab_send.at[v, k], slab_recv.at[v, peer], {"depth": peer}
+            ).wait_recv()
+
+        picture = jnp.zeros((channels - 1, group_rows, width), jnp.float32)
+        cover = jnp.zeros((group_rows, width), jnp.float32)
         passing = jnp.ones((group_rows, width), jnp.float32)
         for q in range(slabs):
-            layer = recv[v][order[v, q]].astype(jnp.float32)
-            picture = picture + passing[None] * layer
-            passing = passing * (1.0 - layer[channels - 1])
-        image[v] = picture
+            slot = order[v, q]
+            dense = recv_alpha[slot, v].astype(jnp.float32)
+            picture = picture + passing[None] * recv[v][slot].astype(jnp.float32)
+            cover = cover + passing * dense
+            passing = passing * (1.0 - dense)
+        image[v, : channels - 1] = picture
+        image[v, channels - 1] = cover
+
+
+def used_rows(rows):
+    last = math.floor(MAX_ZOOM * (rows - 1) + MAX_SHIFT) + 1
+    return min(rows, -(-(last + 1) // 8) * 8)
 
 
 def local(slabs, tiles, density, view_zoom, view_shift, tf_weights, perm_order):
@@ -284,6 +333,7 @@
     group_rows = rows // slabs
     matrices, tap_total = constants(cells, rows, width)
     vmem = pl.BlockSpec(memory_space=pltpu.VMEM)
+    hbm = pl.BlockSpec(memory_space=pl.ANY)
     smem = pl.BlockSpec(memory_space=pltpu.SMEM)
     bf16 = jnp.bfloat16
     block = pltpu.VMEM((cells, rows, width), bf16)
@@ -292,19 +342,24 @@
     return pl.pallas_call(
         functools.partial(kernel, slabs, tiles, tap_total),
         out_shape=jax.ShapeDtypeStruct((views, channels, group_rows, width), jnp.float32),
-        in_specs=[vmem, smem, smem, smem, smem] + [vmem] * len(matrices),
+        in_specs=[hbm, smem, smem, smem, smem] + [hbm] * len(matrices),
         out_specs=vmem,
-        scratch_shapes=[
+        scratch_shapes=[block]
+        + [pltpu.VMEM(m.shape, bf16) for m in matrices]
+        + [
             pltpu.VMEM((views * rows, rows), bf16),
             edge, edge, edge,
             block, block, block,
             pltpu.VMEM((cells, views * rows, width), jnp.float32),
             pltpu.VMEM((views, channels - 1, cells, rows, width), jnp.float32),
             block,
-            pltpu.VMEM((views, slabs, channels, group_rows, width), bf16),
+            pltpu.VMEM((slabs, views, group_rows, width), bf16),
+            pltpu.VMEM((views, slabs, channels - 1, group_rows, width), bf16),
+            pltpu.VMEM((slabs, views, group_rows, width), bf16),
         ]
-        + [pltpu.VMEM((slabs, channels, group_rows, width), bf16)] * views
-        + [dma((2,)), dma((2,)), dma((2,)), dma((2,)), dma((views, slabs)), dma((views, slabs))],
+        + [pltpu.VMEM((slabs, channels - 1, group_rows, width), bf16)] * views
+        + [dma((1 + len(matrices),)), dma((2,)), dma((2,)), dma((2,)), dma((2,)), dma((slabs,)), dma((slabs,))]
+        + [dma((views, slabs)), dma((views, slabs))],
         compiler_params=pltpu.CompilerParams(
             collective_id=0, has_side_effects=True, vmem_limit_bytes=60 * 1024 * 1024
         ),

time: 37.6 us -> 36.3 us (0.965)
  Pallas kernels: 35.8 us -> 34.4 us
    pallas_call x1, Pallas kernels: 35.8 us -> 34.4 us  [local(): pl.pallas_call(functools.partial(kernel, slabs, tiles, tap_total), out_sh...]
where the time goes in v2:
time: 36.3 us; the launch traced here: 36.1 us
  Pallas kernels  34.4 us (95%)
  local copies, waits for them, and re-layouts  1.67 us (5%)
    pallas_call x1, Pallas kernels, local(): pl.pallas_call(functools.partial(kernel, slabs, tiles, tap_total), out_sh...  34.4 us
    unnamed x1, local copies, waits for them, and re-layouts  1.67 us

profile of v2, /device:TPU:4, one launch (start us, length us, event | category | flops | bytes accessed | tf_op | source)
XLA Modules:
  0.0 36.1 jit_solution(11959172902567755273)
XLA Ops:
  0.0 34.4 %shard_map.100 = f32[2,4,64,128]{3,2,1,0:T(8,128)} custom-call(bf16[8,256,128]{2,1,0:T(8,128)(2,1)} %density_in.1, f32[2]{0:T(128)} %zoom.1, f32[2]{0:T(128)} %shift.1, f32[2,4,8]{2,1,0:T(4,128)} %weights.1, s32[2,4]{1,0:T(2,128)} %order.1, bf16[1024,128]{1,0:T(8,128)(2,1)} %constant.10.clone.pack_in, bf16[128,128]{1,0:T(8,128)(2,1)} %constant.11.clone.width_in, ...), custom_call_target="tpu_custom_call" | custom-call | tf_op jit(solution)/shard_map/pallas_call | solution.py:342
  34.4 1.7 %copy.12 = f32[2,4,64,128]{3,2,1,0:T(8,128)} copy(f32[2,4,64,128]{3,2,1,0:T(8,128)} %shard_map.100) | data formatting | bytes 524288

commit v3 on v2

--- a/solution.py
+++ b/solution.py
@@ -12,8 +12,6 @@
 RADIUS = 8
 OCCLUSION_GAIN = 1.5
 EXTINCTION = 0.5
-MAX_ZOOM = 0.9
-MAX_SHIFT = 16.0
 LOG2E = math.log2(math.e)
 GROUP = 16
 CHUNK = 32
@@ -46,7 +44,7 @@
             pack[z, width - RADIUS + j, half + z * RADIUS + j] = 1.0
         low[half + z * RADIUS : half + (z + 1) * RADIUS, z] = from_low
         high[z * RADIUS : (z + 1) * RADIUS, z] = from_high
-    halo = np.concatenate([low, high]).reshape(2 * width, cells * width)
+    halo = (low + high).reshape(width, cells * width)
     depth = np.kron(band(cells, 3 * cells, -cells, taps), np.eye(GROUP))
     arrays = (
         pack.reshape(cells * width, width),
@@ -67,13 +65,13 @@
     density_in, zoom, shift, weights, order, pack_in, width_in, halo_in, height_in, depth_in,
     image,
     density, pack_m, width_m, halo_m, height_m, depth_m,
-    table, packed, from_left, from_right, plane, from_low, from_high, sampled, lit, shade, alpha, slab, recv_alpha, *rest,
+    table, packed, from_left, from_right, edges, edges_low, edges_high,
+    plane, plane_low, plane_high, from_low, from_high, sampled, lit, shade, alpha, slab, recv_alpha, *rest,
 ):
     views, channels, basis = weights.shape
     cells, rows, width = density_in.shape
-    used = used_rows(rows)
     recv = rest[:views]
-    fetch_sem, tile_send, tile_recv, depth_send, depth_recv, alpha_send, alpha_recv, slab_send, slab_recv = rest[views:]
+    fetch_sem, tile_send, tile_recv, depth_send, depth_recv, edge_send, edge_recv, alpha_send, alpha_recv, slab_send, slab_recv = rest[views:]
     group_rows = rows // slabs
     d = lax.axis_index("depth")
     t = lax.axis_index("tile")
@@ -122,6 +120,9 @@
         barrier, slabs - 1 + (t > 0).astype(jnp.int32) + (t < tiles - 1).astype(jnp.int32)
     )
 
+    to_below = remote(density, from_high, depth_send.at[0], depth_recv.at[1], {"depth": d - 1})
+    to_above = remote(density, from_low, depth_send.at[1], depth_recv.at[0], {"depth": d + 1})
+
     @pl.when(t > 0)
     def _():
         to_left.start()
@@ -130,6 +131,14 @@
     def _():
         to_right.start()
 
+    @pl.when(d > 0)
+    def _():
+        to_below.start()
+
+    @pl.when(d < slabs - 1)
+    def _():
+        to_above.start()
+
     @pl.when(t == 0)
     def _():
         from_left[...] = jnp.zeros_like(from_left)
@@ -138,17 +147,15 @@
     def _():
         from_right[...] = jnp.zeros_like(from_right)
 
-    if used < rows:
-        from_low[:, used:] = jnp.zeros((cells, rows - used, width), bf16)
-        from_high[:, used:] = jnp.zeros((cells, rows - used, width), bf16)
-
     @pl.when(d == 0)
     def _():
         from_low[...] = jnp.zeros_like(from_low)
+        edges_low[...] = jnp.zeros_like(edges_low)
 
     @pl.when(d == slabs - 1)
     def _():
         from_high[...] = jnp.zeros_like(from_high)
+        edges_high[...] = jnp.zeros_like(edges_high)
 
     pixel = lax.broadcasted_iota(jnp.int32, (rows, rows), 0).astype(jnp.float32)
     cell = lax.broadcasted_iota(jnp.int32, (rows, rows), 1).astype(jnp.float32)
@@ -165,7 +172,6 @@
     resample(density)
     for fetch in fetches[2:]:
         fetch.wait()
-    inner = matmul(density[...].reshape(cells * rows, width), width_m[...])
 
     @pl.when(t > 0)
     def _():
@@ -177,25 +183,34 @@
         to_right.wait_send()
         to_left.wait_recv()
 
-    outer = matmul(jnp.concatenate([from_left[...], from_right[...]], axis=1), halo_m[...])
-    along_width = jnp.concatenate(
-        [inner[z * rows : (z + 1) * rows] + outer[:, z * width : (z + 1) * width] for z in range(cells)],
-        axis=1,
+    lane = lax.broadcasted_iota(jnp.int32, (rows, width), 1)
+    edges[...] = jnp.where(
+        lane < cells * RADIUS, from_right[...].astype(jnp.float32), from_left[...].astype(jnp.float32)
     ).astype(bf16)
-    flat = matmul(height_m[...], along_width).astype(bf16)
-    for z in range(cells):
-        plane[z] = flat[:, z * width : (z + 1) * width]
-
-    to_below = remote(plane.at[:, :used], from_high.at[:, :used], depth_send.at[0], depth_recv.at[1], {"depth": d - 1})
-    to_above = remote(plane.at[:, :used], from_low.at[:, :used], depth_send.at[1], depth_recv.at[0], {"depth": d + 1})
+
+    def blur_plane(block, sides, out):
+        inner = matmul(block[...].reshape(cells * rows, width), width_m[...])
+        outer = matmul(sides[...], halo_m[...])
+        along_width = jnp.concatenate(
+            [inner[z * rows : (z + 1) * rows] + outer[:, z * width : (z + 1) * width] for z in range(cells)],
+            axis=1,
+        ).astype(bf16)
+        flat = matmul(height_m[...], along_width).astype(bf16)
+        for z in range(cells):
+            out[z] = flat[:, z * width : (z + 1) * width]
+
+    edges_below = remote(edges, edges_high, edge_send.at[0], edge_recv.at[1], {"depth": d - 1})
+    edges_above = remote(edges, edges_low, edge_send.at[1], edge_recv.at[0], {"depth": d + 1})
 
     @pl.when(d > 0)
     def _():
-        to_below.start()
+        edges_below.start()
 
     @pl.when(d < slabs - 1)
     def _():
-        to_above.start()
+        edges_above.start()
+
+    blur_plane(density, edges, plane)
 
     chunk = min(CHUNK, group_rows)
     per_group = group_rows // chunk
@@ -235,16 +250,6 @@
 
         lax.fori_loop(0, rows // chunk, transfer, 0)
 
-    @pl.when(d > 0)
-    def _():
-        to_below.wait_send()
-        to_above.wait_recv()
-
-    @pl.when(d < slabs - 1)
-    def _():
-        to_above.wait_send()
-        to_below.wait_recv()
-
     def peer_of(k):
         return lax.rem(d + k, slabs)
 
@@ -256,12 +261,28 @@
         alpha_copy(k).start()
     recv_alpha[d] = alpha[d]
 
+    @pl.when(d > 0)
+    def _():
+        to_below.wait_send()
+        to_above.wait_recv()
+        edges_below.wait_send()
+        edges_above.wait_recv()
+
+    @pl.when(d < slabs - 1)
+    def _():
+        to_above.wait_send()
+        to_below.wait_recv()
+        edges_above.wait_send()
+        edges_below.wait_recv()
+
+    blur_plane(from_low, edges_low, plane_low)
+    blur_plane(from_high, edges_high, plane_high)
     gain = -OCCLUSION_GAIN * LOG2E / tap_total**3
     for g in range(0, rows, 2 * GROUP):
         def column(at):
             part = pl.ds(at, GROUP)
             return jnp.concatenate(
-                [ref[:, part, :].reshape(cells * GROUP, width) for ref in (from_low, plane, from_high)], axis=0
+                [ref[:, part, :].reshape(cells * GROUP, width) for ref in (plane_low, plane, plane_high)], axis=0
             )
 
         both = matmul(depth_m[...], jnp.concatenate([column(g), column(g + GROUP)], axis=1))
@@ -320,11 +341,6 @@
             passing = passing * (1.0 - dense)
         image[v, : channels - 1] = picture
         image[v, channels - 1] = cover
-
-
-def used_rows(rows):
-    last = math.floor(MAX_ZOOM * (rows - 1) + MAX_SHIFT) + 1
-    return min(rows, -(-(last + 1) // 8) * 8)
 
 
 def local(slabs, tiles, density, view_zoom, view_shift, tf_weights, perm_order):
@@ -348,8 +364,8 @@
         + [pltpu.VMEM(m.shape, bf16) for m in matrices]
         + [
             pltpu.VMEM((views * rows, rows), bf16),
-            edge, edge, edge,
-            block, block, block,
+            edge, edge, edge, edge, edge, edge,
+            block, block, block, block, block,
             pltpu.VMEM((cells, views * rows, width), jnp.float32),
             pltpu.VMEM((views, channels - 1, cells, rows, width), jnp.float32),
             block,
@@ -358,7 +374,8 @@
             pltpu.VMEM((slabs, views, group_rows, width), bf16),
         ]
         + [pltpu.VMEM((slabs, channels - 1, group_rows, width), bf16)] * views
-        + [dma((1 + len(matrices),)), dma((2,)), dma((2,)), dma((2,)), dma((2,)), dma((slabs,)), dma((slabs,))]
+        + [dma((1 + len(matrices),)), dma((2,)), dma((2,)), dma((2,)), dma((2,)), dma((2,)), dma((2,))]
+        + [dma((slabs,)), dma((slabs,))]
         + [dma((views, slabs)), dma((views, slabs))],
         compiler_params=pltpu.CompilerParams(
             collective_id=0, has_side_effects=True, vmem_limit_bytes=60 * 1024 * 1024

time: 36.3 us -> 34.6 us (0.953)
  the two profiles are of different devices: /device:TPU:4 before, /device:TPU:0 now
where the time goes in v3:
time: 34.6 us; the launch traced here: 34.4 us
  Pallas kernels  32.7 us (95%)
  local copies, waits for them, and re-layouts  1.67 us (5%)
    pallas_call x1, Pallas kernels, local(): pl.pallas_call(functools.partial(kernel, slabs, tiles, tap_total), out_sh...  32.7 us
    unnamed x1, local copies, waits for them, and re-layouts  1.67 us

profile of v3, /device:TPU:0, one launch (start us, length us, event | category | flops | bytes accessed | tf_op | source)
XLA Modules:
  0.0 34.4 jit_solution(14409805317527967440)
XLA Ops:
  0.0 32.7 %shard_map.100 = f32[2,4,64,128]{3,2,1,0:T(8,128)} custom-call(bf16[8,256,128]{2,1,0:T(8,128)(2,1)} %density_in.1, f32[2]{0:T(128)} %zoom.1, f32[2]{0:T(128)} %shift.1, f32[2,4,8]{2,1,0:T(4,128)} %weights.1, s32[2,4]{1,0:T(2,128)} %order.1, bf16[1024,128]{1,0:T(8,128)(2,1)} %constant.10.clone.pack_in, bf16[128,128]{1,0:T(8,128)(2,1)} %constant.11.clone.width_in, ...), custom_call_target="tpu_custom_call" | custom-call | tf_op jit(solution)/shard_map/pallas_call | solution.py:358
  32.7 1.7 %copy.12 = f32[2,4,64,128]{3,2,1,0:T(8,128)} copy(f32[2,4,64,128]{3,2,1,0:T(8,128)} %shard_map.100) | data formatting | bytes 524288

commit v4 on v3

--- a/solution.py
+++ b/solution.py
@@ -63,15 +63,15 @@
 def kernel(
     slabs, tiles, tap_total,
     density_in, zoom, shift, weights, order, pack_in, width_in, halo_in, height_in, depth_in,
-    image,
+    image_out,
     density, pack_m, width_m, halo_m, height_m, depth_m,
     table, packed, from_left, from_right, edges, edges_low, edges_high,
-    plane, plane_low, plane_high, from_low, from_high, sampled, lit, shade, alpha, slab, recv_alpha, *rest,
+    plane, plane_low, plane_high, from_low, from_high, sampled, lit, shade, alpha, slab, recv_alpha, image, *rest,
 ):
     views, channels, basis = weights.shape
     cells, rows, width = density_in.shape
     recv = rest[:views]
-    fetch_sem, tile_send, tile_recv, depth_send, depth_recv, edge_send, edge_recv, alpha_send, alpha_recv, slab_send, slab_recv = rest[views:]
+    fetch_sem, out_sem, tile_send, tile_recv, depth_send, depth_recv, edge_send, edge_recv, alpha_send, alpha_recv, slab_send, slab_recv = rest[views:]
     group_rows = rows // slabs
     d = lax.axis_index("depth")
     t = lax.axis_index("tile")
@@ -120,8 +120,16 @@
         barrier, slabs - 1 + (t > 0).astype(jnp.int32) + (t < tiles - 1).astype(jnp.int32)
     )
 
-    to_below = remote(density, from_high, depth_send.at[0], depth_recv.at[1], {"depth": d - 1})
-    to_above = remote(density, from_low, depth_send.at[1], depth_recv.at[0], {"depth": d + 1})
+    half = cells // 2
+    parts = [slice(0, half), slice(half, cells)]
+    to_below = [
+        remote(density.at[p], from_high.at[p], depth_send.at[0, i], depth_recv.at[1, i], {"depth": d - 1})
+        for i, p in enumerate(parts)
+    ]
+    to_above = [
+        remote(density.at[p], from_low.at[p], depth_send.at[1, i], depth_recv.at[0, i], {"depth": d + 1})
+        for i, p in enumerate(parts)
+    ]
 
     @pl.when(t > 0)
     def _():
@@ -133,11 +141,11 @@
 
     @pl.when(d > 0)
     def _():
-        to_below.start()
+        to_below[0].start()
 
     @pl.when(d < slabs - 1)
     def _():
-        to_above.start()
+        to_above[0].start()
 
     @pl.when(t == 0)
     def _():
@@ -188,16 +196,17 @@
         lane < cells * RADIUS, from_right[...].astype(jnp.float32), from_left[...].astype(jnp.float32)
     ).astype(bf16)
 
-    def blur_plane(block, sides, out):
-        inner = matmul(block[...].reshape(cells * rows, width), width_m[...])
-        outer = matmul(sides[...], halo_m[...])
+    def blur_plane(block, sides, out, part):
+        count = part.stop - part.start
+        inner = matmul(block[part].reshape(count * rows, width), width_m[...])
+        outer = matmul(sides[...], halo_m[:, part.start * width : part.stop * width])
         along_width = jnp.concatenate(
-            [inner[z * rows : (z + 1) * rows] + outer[:, z * width : (z + 1) * width] for z in range(cells)],
+            [inner[z * rows : (z + 1) * rows] + outer[:, z * width : (z + 1) * width] for z in range(count)],
             axis=1,
         ).astype(bf16)
         flat = matmul(height_m[...], along_width).astype(bf16)
-        for z in range(cells):
-            out[z] = flat[:, z * width : (z + 1) * width]
+        for z in range(count):
+            out[part.start + z] = flat[:, z * width : (z + 1) * width]
 
     edges_below = remote(edges, edges_high, edge_send.at[0], edge_recv.at[1], {"depth": d - 1})
     edges_above = remote(edges, edges_low, edge_send.at[1], edge_recv.at[0], {"depth": d + 1})
@@ -205,12 +214,14 @@
     @pl.when(d > 0)
     def _():
         edges_below.start()
+        to_below[1].start()
 
     @pl.when(d < slabs - 1)
     def _():
         edges_above.start()
-
-    blur_plane(density, edges, plane)
+        to_above[1].start()
+
+    blur_plane(density, edges, plane, slice(0, cells))
 
     chunk = min(CHUNK, group_rows)
     per_group = group_rows // chunk
@@ -261,22 +272,26 @@
         alpha_copy(k).start()
     recv_alpha[d] = alpha[d]
 
-    @pl.when(d > 0)
-    def _():
-        to_below.wait_send()
-        to_above.wait_recv()
-        edges_below.wait_send()
-        edges_above.wait_recv()
-
-    @pl.when(d < slabs - 1)
-    def _():
-        to_above.wait_send()
-        to_below.wait_recv()
-        edges_above.wait_send()
-        edges_below.wait_recv()
-
-    blur_plane(from_low, edges_low, plane_low)
-    blur_plane(from_high, edges_high, plane_high)
+    for i, part in enumerate(parts):
+        @pl.when(d > 0)
+        def _():
+            to_below[i].wait_send()
+            to_above[i].wait_recv()
+            if i == 0:
+                edges_below.wait_send()
+                edges_above.wait_recv()
+
+        @pl.when(d < slabs - 1)
+        def _():
+            to_above[i].wait_send()
+            to_below[i].wait_recv()
+            if i == 0:
+                edges_above.wait_send()
+                edges_below.wait_recv()
+
+        blur_plane(from_low, edges_low, plane_low, part)
+        blur_plane(from_high, edges_high, plane_high, part)
+
     gain = -OCCLUSION_GAIN * LOG2E / tap_total**3
     for g in range(0, rows, 2 * GROUP):
         def column(at):
@@ -341,6 +356,10 @@
             passing = passing * (1.0 - dense)
         image[v, : channels - 1] = picture
         image[v, channels - 1] = cover
+        pltpu.make_async_copy(image.at[v], image_out.at[v], out_sem.at[v]).start()
+
+    for v in range(views):
+        pltpu.make_async_copy(image.at[v], image_out.at[v], out_sem.at[v]).wait()
 
 
 def local(slabs, tiles, density, view_zoom, view_shift, tf_weights, perm_order):
@@ -348,7 +367,6 @@
     views, channels, _ = tf_weights.shape
     group_rows = rows // slabs
     matrices, tap_total = constants(cells, rows, width)
-    vmem = pl.BlockSpec(memory_space=pltpu.VMEM)
     hbm = pl.BlockSpec(memory_space=pl.ANY)
     smem = pl.BlockSpec(memory_space=pltpu.SMEM)
     bf16 = jnp.bfloat16
@@ -359,7 +377,7 @@
         functools.partial(kernel, slabs, tiles, tap_total),
         out_shape=jax.ShapeDtypeStruct((views, channels, group_rows, width), jnp.float32),
         in_specs=[hbm, smem, smem, smem, smem] + [hbm] * len(matrices),
-        out_specs=vmem,
+        out_specs=hbm,
         scratch_shapes=[block]
         + [pltpu.VMEM(m.shape, bf16) for m in matrices]
         + [
@@ -372,9 +390,10 @@
             pltpu.VMEM((slabs, views, group_rows, width), bf16),
             pltpu.VMEM((views, slabs, channels - 1, group_rows, width), bf16),
             pltpu.VMEM((slabs, views, group_rows, width), bf16),
+            pltpu.VMEM((views, channels, group_rows, width), jnp.float32),
         ]
         + [pltpu.VMEM((slabs, channels - 1, group_rows, width), bf16)] * views
-        + [dma((1 + len(matrices),)), dma((2,)), dma((2,)), dma((2,)), dma((2,)), dma((2,)), dma((2,))]
+        + [dma((1 + len(matrices),)), dma((views,)), dma((2,)), dma((2,)), dma((2, 2)), dma((2, 2)), dma((2,)), dma((2,))]
         + [dma((slabs,)), dma((slabs,))]
         + [dma((views, slabs)), dma((views, slabs))],
         compiler_params=pltpu.CompilerParams(

time: 34.6 us -> 34.4 us (level)
  no operation moved by 1% of the time
where the time goes in v4:
time: 34.4 us; the launch traced here: 34.2 us
  Pallas kernels  32.5 us (94%)
  local copies, waits for them, and re-layouts  1.67 us (5%)
    pallas_call x1, Pallas kernels, local(): pl.pallas_call(functools.partial(kernel, slabs, tiles, tap_total), out_sh...  32.5 us
    unnamed x1, local copies, waits for them, and re-layouts  1.67 us

profile of v4, /device:TPU:0, one launch (start us, length us, event | category | flops | bytes accessed | tf_op | source)
XLA Modules:
  0.0 34.2 jit_solution(6438772498116699475)
XLA Ops:
  0.0 32.5 %shard_map.100 = f32[2,4,64,128]{3,2,1,0:T(8,128)} custom-call(bf16[8,256,128]{2,1,0:T(8,128)(2,1)} %density_in.1, f32[2]{0:T(128)} %zoom.1, f32[2]{0:T(128)} %shift.1, f32[2,4,8]{2,1,0:T(4,128)} %weights.1, s32[2,4]{1,0:T(2,128)} %order.1, bf16[1024,128]{1,0:T(8,128)(2,1)} %constant.10.clone.pack_in, bf16[128,128]{1,0:T(8,128)(2,1)} %constant.11.clone.width_in, ...), custom_call_target="tpu_custom_call" | custom-call | tf_op jit(solution)/shard_map/pallas_call | solution.py:376
  32.5 1.7 %copy.12 = f32[2,4,64,128]{3,2,1,0:T(8,128)} copy(f32[2,4,64,128]{3,2,1,0:T(8,128)} %shard_map.100) | data formatting | bytes 524288

commit v5 on v4

--- a/solution.py
+++ b/solution.py
@@ -102,8 +102,6 @@
     ]
     for fetch in fetches:
         fetch.start()
-    fetches[0].wait()
-    fetches[1].wait()
 
     def remote(src, dst, send, recv_sem, peer):
         return pltpu.make_async_remote_copy(
@@ -111,8 +109,6 @@
             device_id=peer, device_id_type=pl.DeviceIdType.MESH,
         )
 
-    whole = jnp.concatenate([density[z] for z in range(cells)], axis=1)
-    packed[...] = matmul(whole, pack_m[...]).astype(bf16)
     to_left = remote(packed, from_right, tile_send.at[0], tile_recv.at[1], {"tile": t - 1})
     to_right = remote(packed, from_left, tile_send.at[1], tile_recv.at[0], {"tile": t + 1})
 
@@ -123,14 +119,26 @@
     half = cells // 2
     parts = [slice(0, half), slice(half, cells)]
     to_below = [
-        remote(density.at[p], from_high.at[p], depth_send.at[0, i], depth_recv.at[1, i], {"depth": d - 1})
+        remote(density_in.at[p], from_high.at[p], depth_send.at[0, i], depth_recv.at[1, i], {"depth": d - 1})
         for i, p in enumerate(parts)
     ]
     to_above = [
-        remote(density.at[p], from_low.at[p], depth_send.at[1, i], depth_recv.at[0, i], {"depth": d + 1})
+        remote(density_in.at[p], from_low.at[p], depth_send.at[1, i], depth_recv.at[0, i], {"depth": d + 1})
         for i, p in enumerate(parts)
     ]
 
+    @pl.when(d > 0)
+    def _():
+        to_below[0].start()
+
+    @pl.when(d < slabs - 1)
+    def _():
+        to_above[0].start()
+
+    fetches[0].wait()
+    fetches[1].wait()
+    whole = jnp.concatenate([density[z] for z in range(cells)], axis=1)
+    packed[...] = matmul(whole, pack_m[...]).astype(bf16)
     @pl.when(t > 0)
     def _():
         to_left.start()
@@ -138,14 +146,6 @@
     @pl.when(t < tiles - 1)
     def _():
         to_right.start()
-
-    @pl.when(d > 0)
-    def _():
-        to_below[0].start()
-
-    @pl.when(d < slabs - 1)
-    def _():
-        to_above[0].start()
 
     @pl.when(t == 0)
     def _():

time: 34.4 us -> 34.6 us (level)
  no operation moved by 1% of the time
where the time goes in v5:
time: 34.6 us; the launch traced here: 34.4 us
  Pallas kernels  32.7 us (95%)
  local copies, waits for them, and re-layouts  1.67 us (5%)
    pallas_call x1, Pallas kernels, local(): pl.pallas_call(functools.partial(kernel, slabs, tiles, tap_total), out_sh...  32.7 us
    unnamed x1, local copies, waits for them, and re-layouts  1.67 us

profile of v5, /device:TPU:0, one launch (start us, length us, event | category | flops | bytes accessed | tf_op | source)
XLA Modules:
  0.0 34.4 jit_solution(3143739207286042151)
XLA Ops:
  0.0 32.7 %shard_map.100 = f32[2,4,64,128]{3,2,1,0:T(8,128)} custom-call(bf16[8,256,128]{2,1,0:T(8,128)(2,1)} %density_in.1, f32[2]{0:T(128)} %zoom.1, f32[2]{0:T(128)} %shift.1, f32[2,4,8]{2,1,0:T(4,128)} %weights.1, s32[2,4]{1,0:T(2,128)} %order.1, bf16[1024,128]{1,0:T(8,128)(2,1)} %constant.10.clone.pack_in, bf16[128,128]{1,0:T(8,128)(2,1)} %constant.11.clone.width_in, ...), custom_call_target="tpu_custom_call" | custom-call | tf_op jit(solution)/shard_map/pallas_call | solution.py:376
  32.7 1.7 %copy.12 = f32[2,4,64,128]{3,2,1,0:T(8,128)} copy(f32[2,4,64,128]{3,2,1,0:T(8,128)} %shard_map.100) | data formatting | bytes 524288

commit v6 on v4

--- a/solution.py
+++ b/solution.py
@@ -171,13 +171,15 @@
         where_at = zoom[v] * pixel + shift[v]
         table[v * rows : (v + 1) * rows] = jnp.maximum(0.0, 1.0 - jnp.abs(where_at - cell)).astype(bf16)
 
-    def resample(source):
+    def resample(source, v):
+        at = slice(v * rows, (v + 1) * rows)
         for z in range(0, cells, 2):
-            pair = matmul(table[...], jnp.concatenate([source[z], source[z + 1]], axis=1))
-            sampled[z] = pair[:, :width]
-            sampled[z + 1] = pair[:, width:]
-
-    resample(density)
+            pair = matmul(table[at], jnp.concatenate([source[z], source[z + 1]], axis=1))
+            sampled[z, at] = pair[:, :width]
+            sampled[z + 1, at] = pair[:, width:]
+
+    for v in range(views):
+        resample(density, v)
     for fetch in fetches[2:]:
         fetch.wait()
 
@@ -304,7 +306,6 @@
         both = jnp.exp2(gain * both).astype(bf16)
         shade[:, g : g + GROUP, :] = both[:, :width].reshape(cells, GROUP, width)
         shade[:, g + GROUP : g + 2 * GROUP, :] = both[:, width:].reshape(cells, GROUP, width)
-    resample(shade)
 
     def slab_copy(v, k):
         return remote(
@@ -312,6 +313,7 @@
         )
 
     for v in range(views):
+        resample(shade, v)
         for k in others + [0]:
             start = pl.multiple_of(peer_of(k) * group_rows, group_rows)
             for i in range(per_group):

time: 34.4 us -> 34.2 us (level)
  no operation moved by 1% of the time
where the time goes in v6:
time: 34.2 us; the launch traced here: 34 us
  Pallas kernels  32.3 us (94%)
  local copies, waits for them, and re-layouts  1.67 us (5%)
    pallas_call x1, Pallas kernels, local(): pl.pallas_call(functools.partial(kernel, slabs, tiles, tap_total), out_sh...  32.3 us
    unnamed x1, local copies, waits for them, and re-layouts  1.67 us

profile of v6, /device:TPU:0, one launch (start us, length us, event | category | flops | bytes accessed | tf_op | source)
XLA Modules:
  0.0 34.0 jit_solution(11590688120706260894)
XLA Ops:
  0.0 32.3 %shard_map.100 = f32[2,4,64,128]{3,2,1,0:T(8,128)} custom-call(bf16[8,256,128]{2,1,0:T(8,128)(2,1)} %density_in.1, f32[2]{0:T(128)} %zoom.1, f32[2]{0:T(128)} %shift.1, f32[2,4,8]{2,1,0:T(4,128)} %weights.1, s32[2,4]{1,0:T(2,128)} %order.1, bf16[1024,128]{1,0:T(8,128)(2,1)} %constant.10.clone.pack_in, bf16[128,128]{1,0:T(8,128)(2,1)} %constant.11.clone.width_in, ...), custom_call_target="tpu_custom_call" | custom-call | tf_op jit(solution)/shard_map/pallas_call | solution.py:378
  32.3 1.7 %copy.12 = f32[2,4,64,128]{3,2,1,0:T(8,128)} copy(f32[2,4,64,128]{3,2,1,0:T(8,128)} %shard_map.100) | data formatting | bytes 524288
